TPU v7x, 32 devices: a whole 2x2x4 slice. The times are simulated.
32 devices in a mesh: wide: 4 (over z), narrow: 8 (over y, x, core).
Axes of the slice: x: 2, y: 2, z: 4, core: 2. Of those that a mesh axis runs over, the one named last changes fastest.
Arguments:
- saved_inputs: bfloat16 [1024, 5120], P('wide', 'narrow'), may hold values from -6 to 6
- out_grads: bfloat16 [1024, 5120], P('wide', 'narrow'), may hold values from -48 to 48
- seq_ids: int32 [1024], P('wide'), may hold values from 0 to 7, as said below
- seq_counts: int32 [8], P('wide'), may hold values from 64 to 192, as said below
- basis_in: bfloat16 [5120, 5120], P('narrow'), may hold values from -0.078125 to 0.078125
- basis_out: bfloat16 [5120, 5120], P('narrow'), may hold values from -0.078125 to 0.078125
- query_rotated: bfloat16 [5120, 5120], P('narrow', 'wide'), may hold values from -6 to 6
- damping: float32 [], replicated, may hold values from 0.05 to 0.5
Outputs:
- eigenvalues: float32 [5120, 5120], P('narrow', 'wide')
- preconditioned: float32 [5120, 5120], P('narrow', 'wide')
Inputs may be any that keep to these rules, and one draw needn't show every extreme that they name: seq_ids names for each token its sequence; the 256 tokens of block w of the token axis belong to the sequences 2 * w to 2 * w + 1, each having at least one token. seq_counts[s] is the number of tokens whose seq_ids equal s.
All inputs are finite; a program needn't handle non-finite values.
Results may differ from a plain program's by a relative error of at most 0.01.
Values may be sent and summed in bfloat16 or wider, within the bound.
No kernel may reach another device: no remote copies, remote signals or barrier semaphores. Data moves between devices by JAX's collectives and lax.ppermute only.
A program may use at most 128 MiB of HBM per device.

v0:
```python
import jax
import jax.numpy as jnp
from jax import lax
from jax.sharding import PartitionSpec as P


def shards(
    saved_inputs, out_grads, seq_ids, seq_counts, basis_in, basis_out, query_rotated, damping
):
    part_in = jnp.dot(saved_inputs, basis_in, preferred_element_type=jnp.float32)
    part_grad = jnp.dot(out_grads, basis_out, preferred_element_type=jnp.float32)
    rot_in = lax.psum(part_in, "narrow").astype(jnp.bfloat16)
    rot_grad = lax.psum_scatter(part_grad, "narrow", scatter_dimension=1, tiled=True).astype(
        jnp.bfloat16
    )
    seq_local = seq_counts.shape[0]
    tok_local = seq_ids.shape[0]
    offset = lax.axis_index("wide") * seq_local
    member = seq_ids[None, :] - offset == jnp.arange(seq_local, dtype=jnp.int32)[:, None]
    weight = (
        jnp.where(member, 1.0, 0.0).astype(jnp.float32) / seq_counts.astype(jnp.float32)[:, None]
    )
    weighted = (rot_grad.astype(jnp.float32)[None, :, :] * weight[:, :, None]).astype(jnp.bfloat16)
    total_seqs = seq_local * lax.axis_size("wide")
    groups = lax.axis_size("wide")
    all_weighted = lax.all_gather(weighted, "wide", axis=0, tiled=True)
    all_weighted = all_weighted.reshape(groups, seq_local, tok_local, all_weighted.shape[2])
    column_rows = lax.all_to_all(rot_in, "wide", split_axis=1, concat_axis=0, tiled=True)
    column_rows = column_rows.reshape(groups, tok_local, column_rows.shape[1])
    per_seq = jnp.einsum(
        "gsti,gtj->gsij", all_weighted, column_rows, preferred_element_type=jnp.float32
    )
    eigenvalues = jnp.sum(per_seq * per_seq, axis=(0, 1)) / total_seqs
    scaled = (query_rotated.astype(jnp.float32) / (eigenvalues + damping)).astype(jnp.bfloat16)
    width = query_rotated.shape[1]
    in_columns = lax.dynamic_slice_in_dim(basis_in, lax.axis_index("wide") * width, width, 1)
    all_scaled, all_columns = (
        lax.all_gather(scaled, "narrow", axis=0, tiled=True),
        lax.all_gather(in_columns, "narrow", axis=0, tiled=True),
    )
    middle = jnp.dot(basis_out, all_scaled, preferred_element_type=jnp.float32).astype(jnp.bfloat16)
    partial_back = lax.dot_general(
        middle, all_columns, (((1,), (1,)), ((), ())), preferred_element_type=jnp.float32
    )
    preconditioned = lax.psum_scatter(partial_back, "wide", scatter_dimension=1, tiled=True)
    return (eigenvalues, preconditioned)


def solution(mesh):
    return jax.shard_map(
        shards,
        mesh=mesh,
        in_specs=(
            P("wide", "narrow"),
            P("wide", "narrow"),
            P("wide"),
            P("wide"),
            P("narrow", None),
            P("narrow", None),
            P("narrow", "wide"),
            P(),
        ),
        out_specs=(P("narrow", "wide"), P("narrow", "wide")),
        check_vma=False,
    )
```

profile of v0, /device:TPU:0, one launch (start us, length us, event | category | flops | bytes accessed | tf_op | source)
XLA Modules:
  0.0 662.8 jit_solution(4311589889708317204)
XLA Ops:
  7.2 0.0 reduce-scatter.3.cloned.1.call-start
  7.2 0.9 copy-done
  8.1 7.4 %fusion.3 = f32[256,5120]{1,0:T(8,128)} fusion(bf16[256,640]{1,0:T(8,128)(2,1)S(1)} %copy-done, bf16[640,5120]{1,0:T(8,128)(2,1)} %param.13), kind=kOutput, calls=%fused_computation.13 | convolution fusion | flops 1677721600 | bytes 12124160 | tf_op jit(solution)/shard_map/dot_general | solution.py:11
  15.5 0.0 reduce-scatter.3.cloned.1.call-update
  15.5 0.9 copy-done.3
  16.5 7.4 %fusion.4 = f32[256,5120]{1,0:T(8,128)} fusion(bf16[256,640]{1,0:T(8,128)(2,1)S(1)} %copy-done.3, bf16[640,5120]{1,0:T(8,128)(2,1)} %param.12), kind=kOutput, calls=%fused_computation.14 | convolution fusion | flops 1677721600 | bytes 12124160 | tf_op jit(solution)/shard_map/dot_general | solution.py:10
  23.9 130.5 %all-reduce.1 = bf16[256,5120]{1,0:T(8,128)(2,1)S(1)} all-reduce(f32[256,5120]{1,0:T(8,128)} %fusion.4), channel_id=1, replica_groups=mesh['wide'=4,'narrow'=8] {'narrow'}, use_global_device_ids=true, to_apply=%region_1.0 | all-reduce | flops 1310720 | bytes 7864320 | tf_op jit(solution)/shard_map/psum | solution.py:12
  154.3 1.7 copy.17
  156.0 5.1 all-to-all-start
  161.1 0.1 fusion.2
  161.2 1.1 convert_convert_fusion
  162.3 1.0 multiply_convert_fusion
  163.3 0.0 all-gather.6.cloned.1.call-start
  164.0 97.9 %all-to-all-done = bf16[256,4,1280]{2,0,1:T(8,128)(2,1)S(1)} async-done(((bf16[256,4,1280]{2,0,1:T(8,128)(2,1)}), bf16[256,4,1280]{2,0,1:T(8,128)(2,1)S(1)}, u32[]{:S(2)}, u32[]{:S(2)}) %all-to-all-start) | async-done | bytes 2621472 | tf_op jit(solution)/shard_map/all_to_all | solution.py:28
  261.9 6.7 %multiply_reduce_fusion = f32[640,1280]{1,0:T(8,128)S(1)} fusion(bf16[4,2,256,640]{3,2,1,0:T(8,128)(2,1)} %bitcast.30, bf16[256,4,1280]{2,0,1:T(8,128)(2,1)S(1)} %all-to-all-done), kind=kOutput, calls=%fused_computation | convolution fusion | flops 3367731200 | bytes 8519680 | tf_op jit(solution)/shard_map/gsti,gtj->gsij/dot_general | solution.py:30
  268.6 2.9 divide_convert_fusion
  271.5 0.0 all-gather.8.cloned.1.call-start
  271.5 2.7 constant_dynamic-slice_fusion
  274.3 0.2 reduce-scatter.5.cloned.1.call-start
  274.5 70.8 %all-gather.6.cloned.1.call-done = bf16[5120,1280]{1,0:T(8,128)(2,1)} async-done(((bf16[640,1280]{1,0:T(8,128)(2,1)}), bf16[5120,1280]{1,0:T(8,128)(2,1)}) %all-gather.6.cloned.1.call-update) | async-done | bytes 13107216 | tf_op jit(solution)/shard_map/all_gather | solution.py:38
  345.3 15.3 %convolution_convert_fusion.clone.4 = bf16[1280,640]{1,0:T(8,128)(2,1)S(1)} fusion(bf16[5120,1280]{1,0:T(8,128)(2,1)} %all-gather.6.cloned.1.call-done, bf16[640,5120]{1,0:T(8,128)(2,1)} %param.13), kind=kOutput, calls=%fused_computation.2.clone.clone.clone.1 | convolution fusion | flops 8389427200 | bytes 21299200 | tf_op jit(solution)/shard_map/dot_general | solution.py:41
  360.6 60.7 %all-gather.8.cloned.1.call-done = bf16[5120,1280]{1,0:T(8,128)(2,1)} async-done(((bf16[640,1280]{1,0:T(8,128)(2,1)}), bf16[5120,1280]{1,0:T(8,128)(2,1)}) %all-gather.8.cloned.1.call-update) | async-done | bytes 13107216 | tf_op jit(solution)/shard_map/all_gather | solution.py:39
  421.2 14.5 %fusion.1 = f32[640,5120]{1,0:T(8,128)} fusion(bf16[5120,1280]{1,0:T(8,128)(2,1)} %all-gather.8.cloned.1.call-done, bf16[1280,640]{1,0:T(8,128)(2,1)S(1)} %convolution_convert_fusion.clone.4), kind=kOutput, calls=%fused_computation.5 | convolution fusion | flops 8388608000 | bytes 27852800 | tf_op jit(solution)/shard_map/dot_general | solution.py:42
  435.8 220.5 %reduce-scatter.5.cloned.1.call-done = f32[640,1280]{1,0:T(8,128)} async-done(((f32[640,5120]{1,0:T(8,128)}), f32[640,1280]{1,0:T(8,128)}) %reduce-scatter.5.cloned.1.call-update) | async-done | bytes 3276816 | tf_op jit(solution)/shard_map/reduce_scatter | solution.py:45
  (19 shorter events, 0.1 us)
Async XLA Ops:
  7.2 1.0 copy-start
  7.2 154.0 %reduce-scatter.3.cloned.1.call-start = ((), (), s32[]{:S(2)}) async-start(), calls=%async_computation.3 | async-start | bytes 5898240 | tf_op jit(solution)/shard_map/reduce_scatter | solution.py:13
  15.5 1.0 copy-start.3
  156.0 5.1 copy-start.5
  156.0 5.1 copy-start.4
  156.0 105.9 %all-to-all-start = ((bf16[256,4,1280]{2,0,1:T(8,128)(2,1)}), bf16[256,4,1280]{2,0,1:T(8,128)(2,1)S(1)}, u32[]{:S(2)}, u32[]{:S(2)}) async-start(bf16[256,4,1280]{2,0,1:T(8,128)(2,1)} %bitcast.28), calls=%async_computation.1 | async-start | bytes 5242880 | tf_op jit(solution)/shard_map/all_to_all | solution.py:28
  161.1 100.8 %all-gather.4.cloned.1.call-start = ((), (), s32[]{:S(2)}) async-start(), calls=%async_computation.4 | async-start | bytes 3276800 | tf_op jit(solution)/shard_map/all_gather | solution.py:26
  163.3 181.9 %all-gather.6.cloned.1.call-start = ((), (), s32[]{:S(2)}) async-start(), calls=%async_computation.5 | async-start | bytes 14745600 | tf_op jit(solution)/shard_map/all_gather | solution.py:38
  261.9 6.7 %copy-start.2 = (bf16[640,1280]{1,0:T(8,128)(2,1)S(1)}, bf16[640,1280]{1,0:T(8,128)(2,1)}, u32[]{:S(2)}) copy-start(bf16[640,1280]{1,0:T(8,128)(2,1)} %param.14) | copy-start | bytes 4915204
  271.5 149.8 %all-gather.8.cloned.1.call-start = ((), (), s32[]{:S(2)}) async-start(), calls=%async_computation.6 | async-start | bytes 14745600 | tf_op jit(solution)/shard_map/all_gather | solution.py:39
  274.3 382.0 %reduce-scatter.5.cloned.1.call-start = ((), (), s32[]{:S(2)}) async-start(), calls=%async_computation.7 | async-start | bytes 16384000 | tf_op jit(solution)/shard_map/reduce_scatter | solution.py:45
  435.8 220.5 %copy-start.1 = (bf16[256,640]{1,0:T(8,128)(2,1)S(1)}, bf16[256,640]{1,0:T(8,128)(2,1)}, u32[]{:S(2)}) copy-start(bf16[256,640]{1,0:T(8,128)(2,1)} %param.9) | copy-start | bytes 983044
Sparse Core Ops, SparseCore 0:
  15.7 80.4 reduce-scatter.2
  164.0 92.1 all-gather.3
  271.6 73.6 all-gather.5
  347.0 74.1 all-gather.7
  435.9 220.3 reduce-scatter.4
where the time goes:
time: 663 us
  waiting for transfers between devices  450 us (68%)
  blocking collectives  130 us (20%)
  matrix products  51.3 us (8%)
  between operations  14.5 us (2%)
    reduce_scatter x1, waiting for transfers between devices, shards(): lax.psum_scatter(partial_back, 'wide', scatter_dimension=1, tiled=True)  220 us
    psum x1, blocking collectives, shards(): rot_in = lax.psum(part_in, 'narrow').astype(jnp.bfloat16)  130 us
    all_to_all x1, waiting for transfers between devices, shards(): lax.all_to_all(rot_in, 'wide', split_axis=1, concat_axis=0, tiled=True)  97.9 us
    all_gather x1, waiting for transfers between devices, shards(): lax.all_gather(scaled, 'narrow', axis=0, tiled=True)  70.8 us
    all_gather x1, waiting for transfers between devices, shards(): lax.all_gather(in_columns, 'narrow', axis=0, tiled=True)  60.7 us
    dot_general x1, matrix products, shards(): jnp.dot(basis_out, all_scaled, preferred_element_type=jnp.float32)  15.3 us
    dot_general x1, matrix products, shards(): lax.dot_general(middle, all_columns, (((1,), (1,)), ((), ())), preferred_...  14.5 us
  transfers between devices with their start and end apart: 6, of which 4 were waited for; matrix products, arithmetic and copies ran while one was open for 4% of the time, Pallas kernels for 0%

commit v1 on v0

--- a/solution.py
+++ b/solution.py
@@ -25,7 +25,10 @@
     groups = lax.axis_size("wide")
     all_weighted = lax.all_gather(weighted, "wide", axis=0, tiled=True)
     all_weighted = all_weighted.reshape(groups, seq_local, tok_local, all_weighted.shape[2])
-    column_rows = lax.all_to_all(rot_in, "wide", split_axis=1, concat_axis=0, tiled=True)
+    column_rows = jnp.concatenate(
+        lax.all_to_all(jnp.stack(jnp.split(rot_in, lax.axis_size("wide"), axis=1)), "wide", 0, 0),
+        axis=0,
+    )
     column_rows = column_rows.reshape(groups, tok_local, column_rows.shape[1])
     per_seq = jnp.einsum(
         "gsti,gtj->gsij", all_weighted, column_rows, preferred_element_type=jnp.float32

time: 663 us -> 664 us (level)
  no operation moved by 1% of the time
where the time goes in v1:
time: 664 us; the launch traced here: 663 us
  waiting for transfers between devices  450 us (68%)
  blocking collectives  130 us (20%)
  matrix products  51.5 us (8%)
  between operations  14.5 us (2%)
  other arithmetic  6.88 us (1%)
    reduce_scatter x1, waiting for transfers between devices, shards(): lax.psum_scatter(partial_back, 'wide', scatter_dimension=1, tiled=True)  220 us
    psum x1, blocking collectives, shards(): rot_in = lax.psum(part_in, 'narrow').astype(jnp.bfloat16)  130 us
    all_to_all x1, waiting for transfers between devices, shards(): lax.all_to_all(jnp.stack(jnp.split(rot_in, lax.axis_size('wide'), axis=1)...  97.9 us
    all_gather x1, waiting for transfers between devices, shards(): lax.all_gather(scaled, 'narrow', axis=0, tiled=True)  70.8 us
    all_gather x1, waiting for transfers between devices, shards(): lax.all_gather(in_columns, 'narrow', axis=0, tiled=True)  60.4 us
    dot_general x1, matrix products, shards(): jnp.dot(basis_out, all_scaled, preferred_element_type=jnp.float32)  15.5 us
    dot_general x1, matrix products, shards(): lax.dot_general(middle, all_columns, (((1,), (1,)), ((), ())), preferred_...  14.5 us
  transfers between devices with their start and end apart: 6, of which 4 were waited for; matrix products, arithmetic and copies ran while one was open for 4% of the time, Pallas kernels for 0%

profile of v1, /device:TPU:0, one launch (start us, length us, event | category | flops | bytes accessed | tf_op | source)
XLA Modules:
  0.0 663.1 jit_solution(15507166695013119454)
XLA Ops:
  7.2 0.0 reduce-scatter.3.cloned.1.call-start
  7.2 0.9 copy-done
  8.1 7.4 %fusion.3 = f32[256,5120]{1,0:T(8,128)} fusion(bf16[256,640]{1,0:T(8,128)(2,1)S(1)} %copy-done, bf16[640,5120]{1,0:T(8,128)(2,1)} %param.13), kind=kOutput, calls=%fused_computation.17 | convolution fusion | flops 1677721600 | bytes 12124160 | tf_op jit(solution)/shard_map/dot_general | solution.py:11
  15.5 0.9 copy-done.3
  16.5 7.4 %fusion.4 = f32[256,5120]{1,0:T(8,128)} fusion(bf16[256,640]{1,0:T(8,128)(2,1)S(1)} %copy-done.3, bf16[640,5120]{1,0:T(8,128)(2,1)} %param.12), kind=kOutput, calls=%fused_computation.18 | convolution fusion | flops 1677721600 | bytes 12124160 | tf_op jit(solution)/shard_map/dot_general | solution.py:10
  23.9 130.5 %all-reduce.1 = bf16[256,5120]{1,0:T(8,128)(2,1)S(1)} all-reduce(f32[256,5120]{1,0:T(8,128)} %fusion.4), channel_id=1, replica_groups=mesh['wide'=4,'narrow'=8] {'narrow'}, use_global_device_ids=true, to_apply=%region_1.0 | all-reduce | flops 1310720 | bytes 7864320 | tf_op jit(solution)/shard_map/psum | solution.py:12
  154.3 0.2 slice_bitcast_fusion.3
  154.5 1.8 pad_maximum_fusion
  156.3 5.1 all-to-all-start
  161.4 0.1 fusion.2
  161.5 1.1 convert_convert_fusion
  162.7 1.0 multiply_convert_fusion
  163.7 0.0 all-gather.6.cloned.1.call-start
  164.4 97.9 %all-to-all-done = bf16[4,256,1280]{2,1,0:T(8,128)(2,1)S(1)} async-done(((bf16[4,256,1280]{2,1,0:T(8,128)(2,1)}), bf16[4,256,1280]{2,1,0:T(8,128)(2,1)S(1)}, u32[]{:S(2)}, u32[]{:S(2)}) %all-to-all-start) | async-done | bytes 2621472 | tf_op jit(solution)/shard_map/all_to_all | solution.py:29
  262.2 6.7 %multiply_reduce_fusion = f32[640,1280]{1,0:T(8,128)S(1)} fusion(bf16[4,2,256,640]{3,2,1,0:T(8,128)(2,1)} %bitcast.31, bf16[4,256,1280]{2,1,0:T(8,128)(2,1)S(1)} %all-to-all-done), kind=kOutput, calls=%fused_computation | convolution fusion | flops 3367731200 | bytes 8519680 | tf_op jit(solution)/shard_map/gsti,gtj->gsij/dot_general | solution.py:33
  268.9 2.9 divide_convert_fusion
  271.8 0.0 all-gather.8.cloned.1.call-start
  271.9 2.7 constant_dynamic-slice_fusion
  274.6 0.2 reduce-scatter.5.cloned.1.call-start
  274.8 70.8 %all-gather.6.cloned.1.call-done = bf16[5120,1280]{1,0:T(8,128)(2,1)} async-done(((bf16[640,1280]{1,0:T(8,128)(2,1)}), bf16[5120,1280]{1,0:T(8,128)(2,1)}) %all-gather.6.cloned.1.call-update) | async-done | bytes 13107216 | tf_op jit(solution)/shard_map/all_gather | solution.py:41
  345.6 15.5 %convolution_convert_fusion.clone.4 = bf16[1280,640]{1,0:T(8,128)(2,1)S(1)} fusion(bf16[5120,1280]{1,0:T(8,128)(2,1)} %all-gather.6.cloned.1.call-done, bf16[640,5120]{1,0:T(8,128)(2,1)} %param.13), kind=kOutput, calls=%fused_computation.2.clone.clone.clone.1 | convolution fusion | flops 8389427200 | bytes 21299200 | tf_op jit(solution)/shard_map/dot_general | solution.py:44
  361.1 60.4 %all-gather.8.cloned.1.call-done = bf16[5120,1280]{1,0:T(8,128)(2,1)} async-done(((bf16[640,1280]{1,0:T(8,128)(2,1)}), bf16[5120,1280]{1,0:T(8,128)(2,1)}) %all-gather.8.cloned.1.call-update) | async-done | bytes 13107216 | tf_op jit(solution)/shard_map/all_gather | solution.py:42
  421.6 14.5 %fusion.1 = f32[640,5120]{1,0:T(8,128)} fusion(bf16[5120,1280]{1,0:T(8,128)(2,1)} %all-gather.8.cloned.1.call-done, bf16[1280,640]{1,0:T(8,128)(2,1)S(1)} %convolution_convert_fusion.clone.4), kind=kOutput, calls=%fused_computation.5 | convolution fusion | flops 8388608000 | bytes 27852800 | tf_op jit(solution)/shard_map/dot_general | solution.py:45
  436.1 220.5 %reduce-scatter.5.cloned.1.call-done = f32[640,1280]{1,0:T(8,128)} async-done(((f32[640,5120]{1,0:T(8,128)}), f32[640,1280]{1,0:T(8,128)}) %reduce-scatter.5.cloned.1.call-update) | async-done | bytes 3276816 | tf_op jit(solution)/shard_map/reduce_scatter | solution.py:48
  (20 shorter events, 0.1 us)
Async XLA Ops:
  7.2 1.0 copy-start
  7.2 154.3 %reduce-scatter.3.cloned.1.call-start = ((), (), s32[]{:S(2)}) async-start(), calls=%async_computation.3 | async-start | bytes 5898240 | tf_op jit(solution)/shard_map/reduce_scatter | solution.py:13
  15.5 1.0 copy-start.3
  156.3 5.1 copy-start.5
  156.3 5.1 copy-start.4
  156.3 105.9 %all-to-all-start = ((bf16[4,256,1280]{2,1,0:T(8,128)(2,1)}), bf16[4,256,1280]{2,1,0:T(8,128)(2,1)S(1)}, u32[]{:S(2)}, u32[]{:S(2)}) async-start(bf16[4,256,1280]{2,1,0:T(8,128)(2,1)} %pad_maximum_fusion), calls=%async_computation.1 | async-start | bytes 5242880 | tf_op jit(solution)/shard_map/all_to_all | solution.py:29
  161.4 100.8 %all-gather.4.cloned.1.call-start = ((), (), s32[]{:S(2)}) async-start(), calls=%async_computation.4 | async-start | bytes 3276800 | tf_op jit(solution)/shard_map/all_gather | solution.py:26
  163.7 181.9 %all-gather.6.cloned.1.call-start = ((), (), s32[]{:S(2)}) async-start(), calls=%async_computation.5 | async-start | bytes 14745600 | tf_op jit(solution)/shard_map/all_gather | solution.py:41
  262.2 6.7 %copy-start.2 = (bf16[640,1280]{1,0:T(8,128)(2,1)S(1)}, bf16[640,1280]{1,0:T(8,128)(2,1)}, u32[]{:S(2)}) copy-start(bf16[640,1280]{1,0:T(8,128)(2,1)} %param.14) | copy-start | bytes 4915204
  271.8 149.8 %all-gather.8.cloned.1.call-start = ((), (), s32[]{:S(2)}) async-start(), calls=%async_computation.6 | async-start | bytes 14745600 | tf_op jit(solution)/shard_map/all_gather | solution.py:42
  274.6 382.0 %reduce-scatter.5.cloned.1.call-start = ((), (), s32[]{:S(2)}) async-start(), calls=%async_computation.7 | async-start | bytes 16384000 | tf_op jit(solution)/shard_map/reduce_scatter | solution.py:48
  436.1 220.5 %copy-start.1 = (bf16[256,640]{1,0:T(8,128)(2,1)S(1)}, bf16[256,640]{1,0:T(8,128)(2,1)}, u32[]{:S(2)}) copy-start(bf16[256,640]{1,0:T(8,128)(2,1)} %param.9) | copy-start | bytes 983044
Sparse Core Ops, SparseCore 0:
  15.7 80.4 reduce-scatter.2
  164.3 92.1 all-gather.3
  271.9 73.6 all-gather.5
  347.3 74.1 all-gather.7
  436.2 220.3 reduce-scatter.4
